TPU v7x, 512 devices: a whole 4x8x8 slice. The times are simulated.
512 devices in a mesh: inner: 32 (over z_lo, y, core), outer: 16 (over x, z_hi).
Axes of the slice: x: 4, y: 8, z: 8 (z_hi: 4, z_lo: 2; z = z_hi * 2 + z_lo), core: 2. Of those that a mesh axis runs over, the one named last changes fastest.
Arguments:
- gradients: bfloat16 [32, 16, 256, 8192], P('inner', 'outer'), may hold values from -6 to 6
- master_shard: float32 [256, 8192], P('outer', 'inner'), may hold values from -6 to 6
- first_moment: float32 [256, 8192], P('outer', 'inner'), may hold values from -48 to 48
- second_moment: float32 [256, 8192], P('outer', 'inner'), may hold values from 100 to 1000
Outputs:
- new_master: float32 [256, 8192], P('outer', 'inner')
- new_first: float32 [256, 8192], P('outer', 'inner')
- new_second: float32 [256, 8192], P('outer', 'inner')
- group_weights: bfloat16 [256, 8192], P(None, 'inner')
All inputs are finite; a program needn't handle non-finite values.
Results may differ from a plain program's by a relative error of at most 0.0025.
Values may be sent and summed in bfloat16 or wider, within the bound.
A program may use at most 64 MiB of HBM per device.

v0:
```python
import jax
import jax.numpy as jnp
from jax import lax
from jax.sharding import PartitionSpec as P

beta_first = 0.9
beta_second = 0.95
learn_rate = 0.05
decay_rate = 0.1
adam_eps = 1e-05
bias_first = 1.0 - 0.9**10
bias_second = 1.0 - 0.95**10


def sum_sources(pieces):
    return jnp.sum(pieces.astype(jnp.float32), axis=0)


def body(gradients, master_shard, first_moment, second_moment):
    local = gradients.reshape(1, gradients.shape[2], gradients.shape[3])
    partial_value = sum_sources(
        lax.all_to_all(local, "inner", split_axis=2, concat_axis=0, tiled=True)
    )
    reduced = sum_sources(
        lax.all_to_all(
            partial_value[None].astype(jnp.bfloat16),
            "outer",
            split_axis=1,
            concat_axis=0,
            tiled=True,
        ).astype(jnp.float32)
    )
    new_first = beta_first * first_moment + (1.0 - beta_first) * reduced
    new_second = beta_second * second_moment + (1.0 - beta_second) * reduced * reduced
    update = (
        new_first / bias_first / (jnp.sqrt(new_second / bias_second) + adam_eps)
        + decay_rate * master_shard
    )
    new_master = master_shard - learn_rate * update
    copy_weights = lax.all_gather(new_master.astype(jnp.bfloat16), "outer", axis=0, tiled=True)
    return (new_master, new_first, new_second, copy_weights)


def solution(mesh):
    return jax.shard_map(
        body,
        mesh=mesh,
        in_specs=(
            P("inner", "outer", None, None),
            P("outer", "inner"),
            P("outer", "inner"),
            P("outer", "inner"),
        ),
        out_specs=(P("outer", "inner"), P("outer", "inner"), P("outer", "inner"), P(None, "inner")),
        check_vma=False,
    )
```

profile of v0, /device:TPU:8, one launch (start us, length us, event | category | flops | bytes accessed | tf_op | source)
XLA Modules:
  0.0 269.7 jit_solution(8920335155351503580)
XLA Ops:
  0.6 17.9 %copy.11 = bf16[1,256,8192]{1,0,2:T(2,128)(2,1)} copy(bf16[1,256,8192]{2,1,0:T(8,128)(2,1)} %bitcast.11) | data formatting | bytes 8388608 | tf_op jit(solution)/shard_map/reshape | solution.py:20
  18.5 0.5 broadcast.18
  19.0 43.5 %reduce.4 = bf16[8192,256]{1,0:T(8,128)(2,1)} reduce(bf16[8192,1,256]{2,1,0:T(2,128)(2,1)} %bitcast.8, bf16[]{:T(256)} %broadcast.18), dimensions={1}, to_apply=%bitcast.4.reduce_sub_computation | reduce | bytes 8388610
  62.5 6.9 %reshape.29 = bf16[32,2,32768]{2,1,0:T(2,128)(2,1)} reshape(bf16[8192,256]{1,0:T(8,128)(2,1)} %reduce.4) | data formatting | bytes 8388608
  69.4 106.8 %all_to_all.21 = bf16[32,2,32768]{2,1,0:T(2,128)(2,1)} all-to-all(bf16[32,2,32768]{2,1,0:T(2,128)(2,1)} %reshape.29), channel_id=1, replica_groups=mesh['inner'=32,'outer'=16] {'inner'}, dimensions={0} | all-to-all | bytes 8388608 | tf_op jit(solution)/shard_map/all_to_all | solution.py:22
  176.2 19.8 %reshape.30 = bf16[8192,1,256]{2,1,0:T(2,128)(2,1)} reshape(bf16[32,2,32768]{2,1,0:T(2,128)(2,1)} %all_to_all.21) | data formatting | bytes 8388608
  196.0 6.1 %copy.16 = bf16[1,256,8192]{1,2,0:T(8,128)(2,1)} copy(bf16[1,256,8192]{1,0,2:T(2,128)(2,1)} %bitcast.9) | data formatting | bytes 8388608
  202.1 0.0 copy-start
  202.1 0.0 copy-start.1
  202.1 0.0 copy-start.2
  202.1 2.8 %reduce_sum.21 = bf16[256,256]{0,1:T(8,128)(2,1)S(1)} reduce(bf16[256,32,256]{0,2,1:T(8,128)(2,1)} %bitcast.10, bf16[]{:T(256)} %constant.4.clone.1), dimensions={1}, to_apply=%region_0.0 | reduce | flops 2031616 | bytes 4325378 | tf_op jit(solution)/shard_map/reduce_sum | solution.py:16
  204.9 0.2 copy.13
  205.1 1.4 reduce.5
  206.6 21.7 %all_to_all.22 = bf16[16,2,2048]{2,1,0:T(2,128)(2,1)S(1)} all-to-all(bf16[16,2,2048]{2,1,0:T(2,128)(2,1)S(1)} %reshape.31), channel_id=1, replica_groups=mesh['inner'=32,'outer'=16] {'outer'}, dimensions={0} | all-to-all | bytes 262144 | tf_op jit(solution)/shard_map/all_to_all | solution.py:25
  228.3 0.1 reshape.32
  228.5 0.0 copy-done
  228.5 0.0 copy-done.1
  228.5 0.0 copy-done.2
  228.5 0.6 fusion.1
  229.1 39.9 %all_gather.3 = bf16[256,256]{1,0:T(8,128)(2,1)S(1)} all-gather(bf16[16,256]{1,0:T(8,128)(2,1)S(1)} %get-tuple-element.4), channel_id=1, replica_groups=mesh['inner'=32,'outer'=16] {'outer'}, dimensions={0}, use_global_device_ids=true | all-gather | bytes 139264 | tf_op jit(solution)/shard_map/all_gather | solution.py:40
  269.0 0.7 copy.19
  (3 shorter events, 0.1 us)
Async XLA Ops:
  202.1 26.4 %copy-start = (f32[16,256]{1,0:T(8,128)S(1)}, f32[16,256]{1,0:T(8,128)}, u32[]{:S(2)}) copy-start(f32[16,256]{1,0:T(8,128)} %param.5) | copy-start | bytes 49156
  202.1 26.4 %copy-start.1 = (f32[16,256]{1,0:T(8,128)S(1)}, f32[16,256]{1,0:T(8,128)}, u32[]{:S(2)}) copy-start(f32[16,256]{1,0:T(8,128)} %param.6) | copy-start | bytes 49156
  202.1 26.4 %copy-start.2 = (f32[16,256]{1,0:T(8,128)S(1)}, f32[16,256]{1,0:T(8,128)}, u32[]{:S(2)}) copy-start(f32[16,256]{1,0:T(8,128)} %param.7) | copy-start | bytes 49156
where the time goes:
time: 271 us; the launch traced here: 270 us
  blocking collectives  168 us (62%)
  local copies, waits for them, and re-layouts  52.1 us (19%)
  other arithmetic  48.4 us (18%)
    all_to_all x1, blocking collectives, body(): lax.all_to_all(local, 'inner', split_axis=2, concat_axis=0, tiled=True)  107 us
    unnamed x2, other arithmetic  44.9 us
    all_gather x1, blocking collectives, body(): lax.all_gather(new_master.astype(jnp.bfloat16), 'outer', axis=0, tiled=True)  39.9 us
    unnamed x14, local copies, waits for them, and re-layouts  34.1 us
    all_to_all x1, blocking collectives, body(): lax.all_to_all(partial_value[None].astype(jnp.bfloat16), 'outer', split_a...  21.7 us
    reshape x1, local copies, waits for them, and re-layouts, body(): local = gradients.reshape(1, gradients.shape[2], gradients.shape[3])  17.9 us

commit v1 on v0

--- a/solution.py
+++ b/solution.py
@@ -12,15 +12,20 @@
 bias_second = 1.0 - 0.95**10
 
 
+def trade_parts(array, axis, split, join):
+    devices = lax.axis_size(axis)
+    blocks = jnp.stack(jnp.split(array, devices, axis=split), axis=0)
+    blocks = lax.all_to_all(blocks, axis, split_axis=0, concat_axis=0)
+    return jnp.concatenate(blocks, axis=join)
+
+
 def sum_sources(pieces):
     return jnp.sum(pieces.astype(jnp.float32), axis=0)
 
 
 def body(gradients, master_shard, first_moment, second_moment):
     local = gradients.reshape(1, gradients.shape[2], gradients.shape[3])
-    partial_value = sum_sources(
-        lax.all_to_all(local, "inner", split_axis=2, concat_axis=0, tiled=True)
-    )
+    partial_value = sum_sources(trade_parts(local, "inner", 2, 0))
     reduced = sum_sources(
         lax.all_to_all(
             partial_value[None].astype(jnp.bfloat16),

time: 271 us -> 191 us (0.70)
  other arithmetic: 48.4 us -> 4.88 us
  local copies, waits for them, and re-layouts: 52.1 us -> 16.9 us
    unnamed x2 -> x1, other arithmetic: 44.9 us -> 1.41 us
    reshape x1 -> x0, local copies, waits for them, and re-layouts: 17.9 us -> none  [body(): local = gradients.reshape(1, gradients.shape[2], gradients.shape[3])]
    unnamed x14 -> x44, local copies, waits for them, and re-layouts: 34.1 us -> 16.7 us
where the time goes in v1:
time: 191 us
  blocking collectives  168 us (88%)
  local copies, waits for them, and re-layouts  16.9 us (9%)
  other arithmetic  4.88 us (3%)
    all_to_all x1, blocking collectives, trade_parts(): blocks = lax.all_to_all(blocks, axis, split_axis=0, concat_axis=0)  106 us
    all_gather x1, blocking collectives, body(): lax.all_gather(new_master.astype(jnp.bfloat16), 'outer', axis=0, tiled=True)  39.9 us
    all_to_all x1, blocking collectives, body(): lax.all_to_all(partial_value[None].astype(jnp.bfloat16), 'outer', split_a...  22.5 us
    unnamed x44, local copies, waits for them, and re-layouts  16.7 us

profile of v1, /device:TPU:8, one launch (start us, length us, event | category | flops | bytes accessed | tf_op | source)
XLA Modules:
  0.0 190.9 jit_solution(15432516116507488973)
XLA Ops:
  0.6 0.0 copy-start
  0.6 1.1 fusion.31
  1.7 1.2 fusion.30
  2.9 0.9 fusion.29
  3.8 0.9 fusion.28
  4.7 0.9 fusion.27
  5.6 0.9 fusion.26
  6.6 0.9 fusion.25
  7.5 0.9 fusion.24
  8.4 0.9 fusion.23
  9.3 0.9 fusion.22
  10.2 0.9 fusion.21
  11.2 0.9 fusion.20
  12.1 0.9 fusion.19
  13.0 0.9 fusion.18
  13.9 0.9 fusion.17
  14.8 0.9 fusion.16
  15.8 0.0 copy-done
  16.2 105.8 %all_to_all.14 = bf16[32,1,256,256]{3,2,1,0:T(8,128)(2,1)} all-to-all(bf16[32,1,256,256]{3,2,1,0:T(8,128)(2,1)S(1)} %fusion), channel_id=1, replica_groups=mesh['inner'=32,'outer'=16] {'inner'}, dimensions={0} | all-to-all | bytes 8388608 | tf_op jit(solution)/shard_map/all_to_all | solution.py:18
  122.0 0.0 copy-start.1
  122.0 0.0 copy-start.2
  122.0 0.0 copy-start.3
  122.0 2.8 %reduce_sum.21 = bf16[256,256]{1,0:T(8,128)(2,1)S(1)} reduce(bf16[32,1,256,256]{3,2,1,0:T(8,128)(2,1)} %all_to_all.14, bf16[]{:T(256)} %constant.4.clone.1), dimensions={0,1}, to_apply=%region_0.0 | reduce | flops 2031616 | bytes 4325378 | tf_op jit(solution)/shard_map/reduce_sum | solution.py:23
  124.9 0.2 copy.11
  125.1 0.5 broadcast.18
  125.6 1.4 reduce.2
  127.0 22.5 %all_to_all.15 = bf16[16,2,2048]{2,1,0:T(2,128)(2,1)S(1)} all-to-all(bf16[16,2,2048]{2,1,0:T(2,128)(2,1)S(1)} %reshape.29), channel_id=1, replica_groups=mesh['inner'=32,'outer'=16] {'outer'}, dimensions={0} | all-to-all | bytes 262144 | tf_op jit(solution)/shard_map/all_to_all | solution.py:30
  149.5 0.1 reshape.30
  149.7 0.0 copy-done.1
  149.7 0.0 copy-done.2
  149.8 0.0 copy-done.3
  149.8 0.6 fusion.33
  150.4 39.9 %all_gather.3 = bf16[256,256]{1,0:T(8,128)(2,1)S(1)} all-gather(bf16[16,256]{1,0:T(8,128)(2,1)S(1)} %get-tuple-element.4), channel_id=1, replica_groups=mesh['inner'=32,'outer'=16] {'outer'}, dimensions={0}, use_global_device_ids=true | all-gather | bytes 139264 | tf_op jit(solution)/shard_map/all_gather | solution.py:45
  190.3 0.7 copy.44
  (19 shorter events, 0.4 us)
Async XLA Ops:
  0.6 15.1 %copy-start = (bf16[1,1,256,8192]{3,2,1,0:T(8,128)(2,1)S(1)}, bf16[1,1,256,8192]{3,2,1,0:T(8,128)(2,1)}, u32[]{:S(2)}) copy-start(bf16[1,1,256,8192]{3,2,1,0:T(8,128)(2,1)} %param.4) | copy-start | bytes 12582916
  122.0 27.7 %copy-start.1 = (f32[16,256]{1,0:T(8,128)S(1)}, f32[16,256]{1,0:T(8,128)}, u32[]{:S(2)}) copy-start(f32[16,256]{1,0:T(8,128)} %param.5) | copy-start | bytes 49156
  122.0 27.7 %copy-start.2 = (f32[16,256]{1,0:T(8,128)S(1)}, f32[16,256]{1,0:T(8,128)}, u32[]{:S(2)}) copy-start(f32[16,256]{1,0:T(8,128)} %param.6) | copy-start | bytes 49156
  122.0 27.7 %copy-start.3 = (f32[16,256]{1,0:T(8,128)S(1)}, f32[16,256]{1,0:T(8,128)}, u32[]{:S(2)}) copy-start(f32[16,256]{1,0:T(8,128)} %param.7) | copy-start | bytes 49156
